TPU v7x, 512 devices: a whole 4x4x16 slice. The times are simulated.
512 devices in a mesh: gx: 16 (over z), gy: 4 (over x), gz: 8 (over y, core).
Axes of the slice: x: 4, y: 4, z: 16, core: 2. Of those that a mesh axis runs over, the one named last changes fastest.
Arguments:
- targets: float32 [3, 524288], P(None, ('gx', 'gy', 'gz')), may hold values from -20 to 20
- sources: float32 [65536, 4, 256], P(('gx', 'gy', 'gz')), may hold values from -20 to 20, as said below
- send_ids: int32 [512, 128, 2], P(('gx', 'gy', 'gz')), may hold values from 0 to 127, as said below
- send_count: int32 [512, 128], P(('gx', 'gy', 'gz')), may hold values from 0 to 2
- far_ids: int32 [4096, 64], P(('gx', 'gy', 'gz')), may hold values from 0 to 65535
- near_ids: int32 [4096, 8], P(('gx', 'gy', 'gz')), may hold values from 0 to 383, as said below
- near_count: int32 [4096], P(('gx', 'gy', 'gz')), may hold values from 1 to 8
Outputs:
- potential: float32 [524288], P(('gx', 'gy', 'gz'))
Inputs may be any that keep to these rules, and one draw needn't show every extreme that they name: `sources`: coordinates of rows 0 to 2; masses in row 3 lie between 0.0002 and 0.002. send_ids of a domain name its own buckets, counted from 0. `near_ids`: entries may name empty slots; the live entries of every near list include a filled slot received from a peer.
All inputs are finite; a program needn't handle non-finite values.
Results may differ from a plain program's by a relative error of at most 0.0003.
Values sent between devices are 32-bit elements; how exact they have to be, the bound alone decides.
A program may use at most 128 MiB of HBM per device.

v0:
```python
import functools

import jax
import jax.numpy as jnp
from jax import lax
from jax.experimental import pallas as pl
from jax.experimental.pallas import tpu as pltpu
from jax.sharding import PartitionSpec as P

ALL = ("gx", "gy", "gz")
MESH = pl.DeviceIdType.MESH
SOFT = 0.01
FAR = 64
NEAR = 8
LISTED = FAR + NEAR
PARAMS = 16
LIMIT = 16 * 1024 * 1024
OWN = 20
AWAY = 28
VMEM = pltpu.VMEM
SMEM = pltpu.SMEM


def iota(shape, dim):
    return lax.broadcasted_iota(jnp.int32, shape, dim)


def sorted_lists(nx, nz, cells_per_x, own, ids, counts):
    lane = iota((8, 128), 1)
    sub = iota((8, 128), 0)
    is_far = lane < FAR
    is_near = (lane >= FAR) & (lane < LISTED)
    remote = ids - own
    rank = remote >> 1
    live = lane - FAR < counts
    near_code = sub * 128 + jnp.where(remote >= 0, (rank % nz) * 2 + (remote & 1), ids)
    holder = jnp.where(remote >= 0, rank // nz, nx)
    cell = ids % cells_per_x
    cell = cell - (cell & 63) + ((cell & 7) << 3) + ((cell >> 3) & 7)
    order = jnp.where(is_far, lane, sub * NEAR + lane - FAR)
    key = jnp.where(is_far, ids // cells_per_x, jnp.where(live, holder, nx + 1)) * 64 + order
    far_base, near_base, most_base = LISTED, LISTED + nx + 1, LISTED + 2 * nx + 3
    far_limit = jnp.where((lane >= far_base) & (lane < near_base), (lane - far_base) * 64, 0)
    near_limit = jnp.where((lane >= near_base) & (lane < most_base), (lane - near_base) * 64, 0)
    zero = jnp.zeros((8, 128), jnp.int32)
    far_place, near_place, far_start, near_start = zero, zero, zero, zero
    for e in range(FAR):
        other = jnp.broadcast_to(key[:, e : e + 1], (8, 128))
        far_place += jnp.where(other < key, 1, 0)
        far_start += jnp.where(other < far_limit, 1, 0)
    for e in range(NEAR):
        other = jnp.broadcast_to(key[:, FAR + e : FAR + e + 1], (8, 128))
        near_start += jnp.where(other < near_limit, 1, 0)
        for r in range(8):
            moved = pltpu.roll(other, r, 0) if r else other
            near_place += jnp.where(moved < key, 1, 0)
    both = jnp.where(is_far, far_place * 8192 + cell, near_place * 8192 + near_code)
    far_list, near_list = zero, zero
    for e in range(LISTED):
        entry = jnp.broadcast_to(both[:, e : e + 1], (8, 128))
        term = jnp.where((entry >> 13) == lane, entry & 8191, 0)
        if e < FAR:
            far_list += term
        else:
            near_list += term
    near_list = jnp.broadcast_to(jnp.sum(near_list, axis=0, keepdims=True), (8, 128))
    near_start = jnp.broadcast_to(jnp.sum(near_start, axis=0, keepdims=True), (8, 128))
    near_rows = zero
    for t in range(8):
        near_rows = jnp.where(sub == t, pltpu.roll(near_list, (FAR - 8 * t) % 128, 1), near_rows)
    most = pltpu.roll(far_start, 127, 1) - far_start
    most = jnp.broadcast_to(jnp.max(most, axis=0, keepdims=True), (8, 128))
    most = pltpu.roll(most, most_base - far_base, 1)
    out = jnp.where(is_far, far_list, jnp.where(is_near, near_rows, far_start + near_start))
    return jnp.where(lane >= most_base, most, out)


def cell_row(x, y, z, m):
    lane = iota((8, 128), 1)
    sub = iota((8, 128), 0)

    def total(*v):
        return jnp.sum(sum(p * q for p, q in zip(*v)) if len(v) == 2 else sum(v[0]), axis=1, keepdims=True)

    mass = total(m)
    cx, cy, cz = (total(v, m) / mass for v in (x, y, z))
    dx, dy, dz = ([h - c for h in v] for v, c in ((x, cx), (y, cy), (z, cz)))
    wx, wy, wz = ([h * w for h, w in zip(v, m)] for v in (dx, dy, dz))
    sxx, syy, szz = total(wx, dx), total(wy, dy), total(wz, dz)
    sxy, sxz, syz = total(wx, dy), total(wx, dz), total(wy, dz)
    values = (
        mass, cx, cy, cz, 1.5 * sxx, 1.5 * syy, 1.5 * szz,
        3.0 * sxy, 3.0 * sxz, 3.0 * syz, 0.5 * (sxx + syy + szz),
    )
    spread = jnp.zeros((8, 128), jnp.float32)
    for p, value in enumerate(values):
        spread = jnp.where(lane == sub * PARAMS + p, value, spread)
    return jnp.sum(spread, axis=0, keepdims=True)


def wrap(value, size):
    return value & (size - 1) if size & (size - 1) == 0 else lax.rem(value, size)


def gather_kernel(
    sizes, send_ids_hbm, send_count_hbm, near_count_hbm, far_hbm, near_hbm, tgt_hbm, src_hbm,
    t_all, meta_all, tiles_all, cnt_all, table, local, far_out,
    send_ids, send_count, cnt_buf, near_count, far, near, tgt,
    src, ids_buf, tbuf, mbuf, obuf, cbuf, cells_all, rows, meta, own_meta,
    t_send, t_recv, m_send, m_recv, o_send, o_recv, c_send, c_recv, x_send, x_recv, n_send, n_recv,
    own_sem, list_sems, own_list_sem, in_sems,
):
    nx, ny, nz = sizes
    gx, gy, gz = (lax.axis_index(n) for n in ALL)
    own = src.shape[0]
    jump = max(1, nx // 4)
    barrier = pltpu.get_barrier_semaphore()
    loads = [
        pltpu.make_async_copy(source, dest, in_sems.at[n])
        for n, (source, dest) in enumerate((
            (send_ids_hbm, send_ids), (send_count_hbm, send_count),
            (send_count_hbm, cnt_buf), (near_count_hbm, near_count),
            (far_hbm, far), (near_hbm, near), (tgt_hbm, tgt), (src_hbm, src),
        ))
    ]
    for load in loads:
        load.start()
    xs = [wrap(gx + d, nx) for d in range(nx)]
    ys = [wrap(gy + d, ny) for d in range(ny)]
    zs = [wrap(gz + d, nz) for d in range(nz)]
    first = sorted((d for d in range(1, nx) if min(d, nx - d) <= jump), key=lambda d: -min(d, nx - d))
    greeted = [(xs[d], gy, gz) for d in first]
    greeted += [(gx, gy, zs[d]) for d in range(1, nz)]
    greeted += [(gx, ys[d], gz) for d in range(1, ny)]
    for device in greeted:
        pl.semaphore_signal(barrier, inc=1, device_id=device, device_id_type=MESH)

    def sent(source, dest, s_sem, r_sem, device):
        copy = pltpu.make_async_remote_copy(
            src_ref=source, dst_ref=dest, send_sem=s_sem, recv_sem=r_sem,
            device_id=device, device_id_type=MESH,
        )
        copy.start()
        return copy

    def meta_of(ref, i):
        return ref.at[pl.ds(pl.multiple_of(i * 1024, 1024), 1024)]

    for load in loads[:-1]:
        load.wait()
    for t in range(8):
        for c in range(3):
            tbuf[c, t : t + 1, :] = tgt[t, c : c + 1, :]
    ids_buf[...] = jnp.zeros((8, 128), jnp.int32)
    ids_buf[:, 0:FAR] = far[...]
    ids_buf[:, FAR:LISTED] = near[...]
    sub = iota((8, 128), 0)
    counts = jnp.zeros((8, 128), jnp.int32)
    for t in range(8):
        counts = jnp.where(sub == t, near_count[t], counts)
    lists = sorted_lists(nx, nz, ny * nz * own, own, ids_buf[...], counts)
    for t in range(8):
        mbuf[pl.ds(t * 128, 128)] = lists[t]
    to_smem = [pltpu.make_async_copy(mbuf, meta_of(meta, gx), list_sems.at[0])]
    to_smem[0].start()
    own_list = pltpu.make_async_copy(mbuf, own_meta, own_list_sem)
    own_list.start()
    loads[-1].wait()

    def moments(g, carry):
        group = src[pl.ds(g * 8, 8)]
        x, y, z, m = ([group[:, h * 4 + r, :] for h in range(2)] for r in range(4))
        cbuf[pl.ds(g, 1), :] = cell_row(x, y, z, m)
        return carry

    lax.fori_loop(0, own // 8, moments, 0, unroll=2)

    def gather_tiles(dz):
        k = zs[dz]

        def gather_for(i, carry):
            r = i * nz + k
            filled = send_count[0, r]
            for s in range(2):
                obuf[k, i * 2 + s] = jnp.where(filled > s, src[send_ids[s, r]], 0.0)
            return carry

        lax.fori_loop(0, nx, gather_for, 0, unroll=min(nx, 8))

    pl.semaphore_wait(barrier, len(greeted))

    t_copy, m_copy = {}, {}
    for d in first:
        device = (xs[d], gy, gz)
        m_copy[d] = sent(mbuf, meta_of(meta_all, gx), m_send.at[d], m_recv.at[d], device)
        t_copy[d] = sent(tbuf, t_all.at[gx], t_send.at[d], t_recv.at[d], device)
    c_copies = [
        sent(cbuf, cells_all.at[gy, gz], c_send.at[d], c_recv.at[d], (gx, gy, zs[d]))
        for d in range(1, nz)
    ]
    c_copies += [
        sent(cnt_buf, cnt_all.at[gz], n_send.at[d], n_recv.at[d], (gx, gy, zs[d]))
        for d in range(1, nz)
    ]
    cells_all[gy, gz] = cbuf[...]
    o_copies = []
    gather_tiles(1)
    for d in range(1, nz):
        gather_tiles((d + 1) % nz)
        o_copies.append(
            sent(obuf.at[zs[d]], tiles_all.at[gz], o_send.at[d], o_recv.at[d], (gx, gy, zs[d]))
        )
    t_all[gx] = tbuf[...]
    meta_all[pl.ds(pl.multiple_of(gx * 1024, 1024), 1024)] = mbuf[...]
    cnt_all[gz] = cnt_buf[...]
    mine = pltpu.make_async_copy(obuf.at[gz], tiles_all.at[gz], own_sem)
    mine.start()

    own_list.wait()
    n0 = own_meta[LISTED + nx + 1 + nx]
    n1 = own_meta[LISTED + nx + 1 + nx + 1]

    def own_item(j, total):
        e = n0 + j
        p = jnp.minimum(e, 8 * NEAR - 1)
        code = own_meta[((p >> 3) << 7) + FAR + (p & 7)]
        t = code >> 7
        tile = src[jnp.minimum(code & 127, own - 1)]
        row = near_row(tile, *(tbuf[c, pl.ds(t, 1), :] for c in range(3)))
        return total - jnp.where((sub == t) & (e < n1), row, 0.0)

    total = lax.fori_loop(0, OWN // 2, own_item, jnp.zeros((8, 128), jnp.float32), unroll=5)
    for copy in c_copies:
        copy.wait_recv()
    x_copies = [
        sent(cells_all.at[gy], cells_all.at[gy], x_send.at[d], x_recv.at[d], (gx, ys[d], gz))
        for d in range(1, ny)
    ]
    local[...] = lax.fori_loop(OWN // 2, OWN, own_item, total, unroll=5)

    half = nx // 2
    for e in range(1, half - jump + 1):
        up, down = jump + e, nx - jump - e
        for copies, ref, of, s_sems, r_sems in (
            (m_copy, meta_all, meta_of, m_send, m_recv),
            (t_copy, t_all, lambda ref, i: ref.at[i], t_send, t_recv),
        ):
            if e == 1:
                copies[jump].wait_recv()
                copies[nx - jump].wait_recv()
            if e < half - jump or copies is t_copy:
                behind = of(ref, xs[nx - jump])
                copies[up] = sent(behind, behind, s_sems.at[up], r_sems.at[up], (xs[e], gy, gz))
            if e < half - jump or copies is m_copy:
                ahead = of(ref, xs[jump])
                copies[down] = sent(ahead, ahead, s_sems.at[down], r_sems.at[down], (xs[nx - e], gy, gz))

    def listed(d):
        from_d = xs[nx - d]
        copy = pltpu.make_async_copy(meta_of(meta_all, from_d), meta_of(meta, from_d), list_sems.at[d])
        copy.start()
        to_smem.append(copy)

    waited = {jump, nx - jump} if half > jump else set()
    for d in first:
        if d not in waited:
            m_copy[d].wait_recv()
            t_copy[d].wait_recv()
        listed(d)
    for copy in x_copies:
        copy.wait_recv()
    blocks = own // 64

    def expand(n, carry):
        for b in range(blocks):
            cells = cells_all[n // nz, n % nz, b * 8 : b * 8 + 8, :]
            for j in range(8):
                moved = pltpu.roll(cells, 128 - PARAMS * j, 1) if j else cells
                table[pl.ds((n * blocks + b) * 64 + j * 8, 8), :] = moved
        return carry

    lax.fori_loop(0, ny * nz, expand, 0, unroll=4)

    k = iota((128, 128), 0)
    spread = jnp.concatenate(
        [jnp.where(((k & 15) == p) & (k < 48), 1.0, 0.0) for p in range(11)], axis=1
    ).astype(jnp.bfloat16)

    def far_domain(n, carry):
        i = wrap(gx + n, nx)
        bounds = []
        slot = rows.at[n & 1]
        for t in range(8):
            at = i * 1024 + t * 128
            f0 = meta[at + LISTED + gx]
            bounds.append(meta[at + LISTED + gx + 1] - f0)
            for u in range(8):
                slot[t * 8 + u : t * 8 + u + 1, :] = table[pl.ds(meta[at + f0 + u], 1), :]
        high, mid, low = parts(slot[...])
        lane = iota((64, 128), 1)
        packed = jnp.where(
            lane < 16, high, jnp.where(lane < 32, pltpu.roll(mid, 16, 1), pltpu.roll(low, 32, 1))
        )
        wide = jnp.dot(packed.astype(jnp.bfloat16), spread, preferred_element_type=jnp.float32)
        values = []
        for t in range(8):
            tx, ty, tz = (t_all[i, c, t : t + 1, :] for c in range(3))
            p = lambda n: wide[t * 8 : t * 8 + 8, n * 128 : n * 128 + 128]
            values.append(far_value(p, bounds[t], tx, ty, tz))
        far_out[i] = -jnp.concatenate(values, axis=0)
        return carry

    for copy in to_smem:
        copy.wait()
    to_smem.clear()
    low_end = nx - jump
    near_end = low_end + len(first) + 1
    lax.fori_loop(low_end, near_end, far_domain, 0, unroll=2 if nx > 4 else 1)
    if near_end < low_end + nx:
        for d in range(1, nx):
            if d not in first:
                m_copy[d].wait_recv()
                t_copy[d].wait_recv()
                listed(d)
        for copy in to_smem:
            copy.wait()
        lax.fori_loop(near_end, low_end + nx, far_domain, 0, unroll=2 if nx > 4 else 1)
    for copy in o_copies:
        copy.wait()
    for copy in [*t_copy.values(), *m_copy.values(), *c_copies, *x_copies]:
        copy.wait_send()
    mine.wait()


def parts(v):
    high = v.astype(jnp.bfloat16).astype(jnp.float32)
    rest = v - high
    mid = rest.astype(jnp.bfloat16).astype(jnp.float32)
    return high, mid, rest - mid


def near_row(tile, x, y, z):
    sub = iota((8, 128), 0)
    left = jnp.concatenate([*parts(tile), jnp.where(sub < 3, 1.0, tile)], axis=0).T
    picks = []
    for c, row in enumerate((x, y, z)):
        high, mid, low = parts(jnp.broadcast_to(-row, (8, 128)))
        target = jnp.where(sub == 0, high, jnp.where(sub == 1, mid, jnp.where(sub == 2, low, 0.0)))
        for h in range(2):
            one = jnp.where(sub == h * 4 + c, 1.0, 0.0)
            picks.append(jnp.concatenate([one, one, one, target], axis=0))
    right = jnp.concatenate(picks, axis=1).astype(jnp.bfloat16)
    d = jnp.dot(left.astype(jnp.bfloat16), right, preferred_element_type=jnp.float32)
    total = jnp.zeros((8, 128), jnp.float32)
    for h in range(2):
        for s in range(0, 128, 8):
            dx, dy, dz = (
                d[s : s + 8, (2 * c + h) * 128 : (2 * c + h + 1) * 128] for c in range(3)
            )
            inv = lax.rsqrt(dx * dx + dy * dy + dz * dz + SOFT)
            total += inv * jnp.broadcast_to(left[s : s + 8, 27 + 4 * h : 28 + 4 * h], (8, 128))
    return jnp.sum(total, axis=0, keepdims=True)


def far_value(p, live, tx, ty, tz):
    dx, dy, dz = tx - p(1), ty - p(2), tz - p(3)
    r2 = dx * dx + dy * dy + dz * dz + SOFT
    inv = lax.rsqrt(r2)
    inv2 = inv * inv
    quad = dx * (p(4) * dx + p(7) * dy + p(8) * dz) + dy * (p(5) * dy + p(9) * dz) + p(6) * dz * dz
    value = inv * (p(0) + (quad - r2 * p(10)) * (inv2 * inv2))
    return jnp.sum(jnp.where(iota((8, 128), 0) < live, value, 0.0), axis=0, keepdims=True)


def walk_kernel(
    sizes, meta, cnt, t_all, tiles, table, src, out, todo, rows, tile_buf, sem
):
    nx, ny, nz = sizes
    a = lax.axis_index("gx")
    gz = lax.axis_index("gz")
    out[...] = jnp.zeros_like(out)
    near_base = LISTED + nx + 1

    def domain(i, found):
        base = i * 1024
        n0 = meta[base + near_base + a]
        n1 = meta[base + near_base + a + 1]

        @pl.when(meta[base + LISTED + 2 * nx + 3 + a] > 8)
        def _():
            def bucket(t, carry):
                at = base + t * 128
                f0 = meta[at + LISTED + a]
                f1 = meta[at + LISTED + a + 1]
                tx, ty, tz = (t_all[i, c, pl.ds(t, 1), :] for c in range(3))

                def chunk(n, carry):
                    start = f0 + n * 8
                    for u in range(8):
                        rows[u : u + 1, :] = table[pl.ds(meta[at + start + u], 1), :]
                    v = rows[...]
                    p = lambda n: jnp.broadcast_to(v[:, n : n + 1], (8, 128))
                    out[i, pl.ds(t, 1), :] -= far_value(p, f1 - start, tx, ty, tz)
                    return carry

                return lax.fori_loop(1, (f1 - f0 + 7) >> 3, chunk, carry)

            lax.fori_loop(0, 8, bucket, 0)

        def entry(e, found):
            code = meta[base + ((e >> 3) << 7) + FAR + (e & 7)]
            peer, slot = (code & 127) >> 1, code & 1
            todo[found] = (i * 8 + (code >> 7)) * 1024 + peer * (nx * 2) + i * 2 + slot
            return found + jnp.where(cnt[peer * (nx * nz) + i * nz + gz] > slot, 1, 0)

        return lax.fori_loop(n0, n1, entry, found)

    found = lax.fori_loop(0, nx, domain, jnp.int32(0))
    todo[nx * 64 + 1] = found

    def away(n, carry):
        item = todo[n]
        i, t = item >> 13, (item >> 10) & 7
        row = near_row(tiles[item & 1023], *(t_all[i, c, pl.ds(t, 1), :] for c in range(3)))
        out[i, pl.ds(t, 1), :] -= row
        return carry

    lax.fori_loop(AWAY, found, away, 0)
    base = a * 1024

    def own_entry(e, carry):
        code = meta[base + ((e >> 3) << 7) + FAR + (e & 7)]
        t = code >> 7
        copy = pltpu.make_async_copy(src.at[code & 127], tile_buf, sem)
        copy.start()
        copy.wait()
        row = near_row(tile_buf[...], *(t_all[a, c, pl.ds(t, 1), :] for c in range(3)))
        out[a, pl.ds(t, 1), :] -= row
        return carry

    lax.fori_loop(meta[base + near_base + nx] + OWN, meta[base + near_base + nx + 1], own_entry, 0)


def return_kernel(
    sizes, todo, t_all, tiles, part, far_part, local, out, landed, near_rows, mine, send, recv,
):
    nx, ny, nz = sizes
    gx, gy, gz = (lax.axis_index(n) for n in ALL)
    barrier = pltpu.get_barrier_semaphore()
    xs = [wrap(gx + d, nx) for d in range(nx)]
    far_first = sorted(range(1, nx), key=lambda d: -min(d, nx - d))
    for d in far_first:
        pl.semaphore_signal(barrier, inc=1, device_id=(xs[d], gy, gz), device_id_type=MESH)
    lane = iota((8, 128), 1)
    found = todo[nx * 64 + 1]

    def near(j, ids):
        item = jnp.where(j < found, todo[j], 0)
        bucket = item >> 10
        i, t = bucket >> 3, bucket & 7
        row = near_row(tiles[item & 1023], *(t_all[i, c, pl.ds(t, 1), :] for c in range(3)))
        near_rows[pl.ds(j, 1), :] = row
        return jnp.where(lane == j, jnp.where(j < found, bucket, -1), ids)

    near_rows[...] = jnp.zeros_like(near_rows)
    ids = lax.fori_loop(0, AWAY, near, jnp.full((8, 128), -1, jnp.int32), unroll=4)
    pick = jnp.where(iota((nx * 8, 128), 0) == jnp.broadcast_to(ids[0:1], (nx * 8, 128)), 1.0, 0.0)
    placed = sum(
        jnp.dot(pick.astype(jnp.bfloat16), v.astype(jnp.bfloat16), preferred_element_type=jnp.float32)
        for v in parts(near_rows[...])
    )
    mine[...] = part[...] + far_part[...] - placed.reshape(nx, 8, 128)

    pl.semaphore_wait(barrier, nx - 1)
    copies = []
    for d in far_first:
        copy = pltpu.make_async_remote_copy(
            src_ref=mine.at[xs[d]], dst_ref=landed.at[d - 1],
            send_sem=send.at[d], recv_sem=recv.at[d],
            device_id=(xs[d], gy, gz), device_id_type=MESH,
        )
        copy.start()
        copies.append(copy)
    summed = mine[gx] + local[...]
    for copy in copies:
        copy.wait()
    for d in range(nx - 1):
        summed += landed[d]
    out[...] = summed


def body(sizes, targets, sources, send_ids, send_count, far_ids, near_ids, near_count):
    nx, ny, nz = sizes
    f32, i32 = jnp.float32, jnp.int32
    own = sources.shape[0]
    shape = jax.ShapeDtypeStruct
    vmem = pl.BlockSpec(memory_space=VMEM)
    smem = pl.BlockSpec(memory_space=SMEM)
    hbm = pl.BlockSpec(memory_space=pltpu.HBM)
    dma = pltpu.SemaphoreType.DMA
    in_hbm = functools.partial(pltpu.with_memory_space_constraint, memory_space=pltpu.HBM)
    tgt = jnp.transpose(targets.reshape(3, 8, 128), (1, 0, 2))
    src = jnp.transpose(sources.reshape(own, 4, 2, 128), (0, 2, 1, 3)).reshape(own, 8, 128)
    t_all, meta, tiles_all, cnt, table, local, far_part = pl.pallas_call(
        functools.partial(gather_kernel, sizes),
        out_shape=(
            shape((nx, 3, 8, 128), f32), shape((nx * 1024,), i32),
            shape((nz, nx * 2, 8, 128), f32), shape((nz, 1, nx * nz), i32),
            shape((ny * nz * own, 128), f32),
            shape((8, 128), f32), shape((nx, 8, 128), f32),
        ),
        in_specs=[hbm] * 7,
        out_specs=(vmem,) * 7,
        scratch_shapes=[
            SMEM((2, nx * nz), i32), SMEM((1, nx * nz), i32), VMEM((1, nx * nz), i32),
            SMEM((8,), i32),
            VMEM((8, FAR), i32), VMEM((8, NEAR), i32), VMEM((8, 3, 128), f32),
            VMEM((own, 8, 128), f32),
            VMEM((8, 128), i32), VMEM((3, 8, 128), f32), VMEM((1024,), i32),
            VMEM((nz, nx * 2, 8, 128), f32), VMEM((own // 8, 128), f32),
            VMEM((ny, nz, own // 8, 128), f32), VMEM((2, 64, 128), f32),
            SMEM((nx * 1024,), i32), SMEM((1024,), i32),
            dma((nx,)), dma((nx,)), dma((nx,)), dma((nx,)), dma((nz,)), dma((nz,)),
            dma((nz,)), dma((nz,)), dma((ny,)), dma((ny,)), dma((nz,)), dma((nz,)),
            dma, dma((nx,)), dma, dma((8,)),
        ],
        compiler_params=pltpu.CompilerParams(
            collective_id=0, has_side_effects=True, vmem_limit_bytes=LIMIT
        ),
        name="gather",
    )(*map(in_hbm, (send_ids[0].T, send_count, near_count, far_ids, near_ids, tgt, src)))

    tiles = tiles_all.reshape(nz * nx * 2, 8, 128)
    part, todo = pl.pallas_call(
        functools.partial(walk_kernel, sizes),
        out_shape=(shape((nx, 8, 128), f32), shape((nx * 64 + 2,), i32)),
        in_specs=[smem, smem, vmem, vmem, vmem, hbm],
        out_specs=(vmem, smem),
        scratch_shapes=[VMEM((8, 128), f32), VMEM((8, 128), f32), dma],
        compiler_params=pltpu.CompilerParams(vmem_limit_bytes=LIMIT),
        name="walk",
    )(meta, cnt.reshape(-1), t_all, tiles, table, in_hbm(src))

    out = pl.pallas_call(
        functools.partial(return_kernel, sizes),
        out_shape=shape((8, 128), f32),
        in_specs=[smem, vmem, vmem, vmem, vmem, vmem],
        out_specs=vmem,
        scratch_shapes=[
            VMEM((nx - 1, 8, 128), f32), VMEM((128, 128), f32),
            VMEM((nx, 8, 128), f32), dma((nx,)), dma((nx,)),
        ],
        compiler_params=pltpu.CompilerParams(
            collective_id=1, has_side_effects=True, vmem_limit_bytes=LIMIT
        ),
        name="bring_back",
    )(todo, t_all, tiles, part, far_part, local)
    return out.reshape(-1)


def solution(mesh):
    sizes = tuple(mesh.shape[n] for n in ALL)
    in_specs = (
        P(None, ALL), P(ALL, None, None), P(ALL, None, None), P(ALL, None),
        P(ALL, None), P(ALL, None), P(ALL),
    )
    return jax.shard_map(
        functools.partial(body, sizes), mesh=mesh, in_specs=in_specs, out_specs=P(ALL),
        check_vma=False,
    )
```

profile of v0, /device:TPU:8, one launch (start us, length us, event | category | flops | bytes accessed | tf_op | source)
XLA Modules:
  0.0 52.6 jit_solution(11719427082228590302)
XLA Ops:
  0.0 33.8 %gather.1 = (f32[16,3,8,128]{3,2,1,0:T(8,128)S(1)}, s32[16384]{0:T(1024)S(1)}, f32[8,32,8,128]{3,2,1,0:T(8,128)S(1)}, s32[8,1,128]{2,1,0:T(1,128)S(1)}, f32[4096...) custom-call(s32[2,128]{1,0:T(2,128)} %bitcast.21, s32[1,128]{1,0:T(1,128)} %send_count_hbm.1, ...), custom_call_target="tpu_custom_call" | custom-call | tf_op jit(solution)/shard_map/gather/pallas_call | solution.py:504
  33.8 4.1 %walk.1 = (f32[16,8,128]{2,1,0:T(8,128)S(1)}, s32[1026]{0:T(1024)S(1)}) custom-call(s32[16384]{0:T(1024)S(1)} %get-tuple-element.14.meta, s32[1024]{0:T(1024)S(1)} %bitcast.17, f32[16,3,8,128]{3,2,1,0:T(8,128)S(1)} %get-tuple-element.16.t_all, f32[256,8,128]{2,1,0:T(8,128)S(1)} %bitcast.14, f32[4096,128]{1,0:T(8,128)S(1)} %get-tuple-element.18.table, ...), custom_call_target="tpu_custom_call" | custom-call | tf_op jit(solution)/shard_map/walk/pallas_call | solution.py:534
  37.9 14.1 %bring_back.1 = f32[8,128]{1,0:T(8,128)S(1)} custom-call(s32[1026]{0:T(1024)S(1)} %get-tuple-element.19.todo, f32[16,3,8,128]{3,2,1,0:T(8,128)S(1)} %get-tuple-element.16.t_all, f32[256,8,128]{2,1,0:T(8,128)S(1)} %bitcast.15, f32[16,8,128]{2,1,0:T(8,128)S(1)} %get-tuple-element.20.part, f32[16,8,128]{2,1,0:T(8,128)S(1)} %get-tuple-element.21.far_part, ...), custom_call_target="tpu_custom_call" | custom-call | tf_op jit(solution)/shard_map/bring_back/pallas_call | solution.py:544
  52.0 0.6 %copy.10 = f32[1024]{0:T(1024)} copy(f32[1024]{0:T(1024)S(1)} %bitcast.16) | data formatting | bytes 8192
where the time goes:
time: 52.6 us
  Pallas kernels  52 us (99%)
  local copies, waits for them, and re-layouts  0.6 us (1%)
    pallas_call x1, Pallas kernels, body(): pl.pallas_call(functools.partial(gather_kernel, sizes), out_shape=(shape(...  33.8 us
    pallas_call x1, Pallas kernels, body(): pl.pallas_call(functools.partial(return_kernel, sizes), out_shape=shape((...  14.1 us
    pallas_call x1, Pallas kernels, body(): pl.pallas_call(functools.partial(walk_kernel, sizes), out_shape=(shape((n...  4.09 us

commit v1 on v0

--- a/solution.py
+++ b/solution.py
@@ -15,7 +15,7 @@
 LISTED = FAR + NEAR
 PARAMS = 16
 LIMIT = 16 * 1024 * 1024
-OWN = 20
+OWN = 24
 AWAY = 28
 VMEM = pltpu.VMEM
 SMEM = pltpu.SMEM
@@ -104,11 +104,11 @@
 
 def gather_kernel(
     sizes, send_ids_hbm, send_count_hbm, near_count_hbm, far_hbm, near_hbm, tgt_hbm, src_hbm,
-    t_all, meta_all, tiles_all, cnt_all, table, local, far_out,
+    t_all, meta_all, tiles_all, cnt_all, table, far_out, mbuf, src,
     send_ids, send_count, cnt_buf, near_count, far, near, tgt,
-    src, ids_buf, tbuf, mbuf, obuf, cbuf, cells_all, rows, meta, own_meta,
+    ids_buf, tbuf, obuf, cbuf, cells_all, rows, meta,
     t_send, t_recv, m_send, m_recv, o_send, o_recv, c_send, c_recv, x_send, x_recv, n_send, n_recv,
-    own_sem, list_sems, own_list_sem, in_sems,
+    own_sem, list_sems, in_sems,
 ):
     nx, ny, nz = sizes
     gx, gy, gz = (lax.axis_index(n) for n in ALL)
@@ -163,8 +163,6 @@
         mbuf[pl.ds(t * 128, 128)] = lists[t]
     to_smem = [pltpu.make_async_copy(mbuf, meta_of(meta, gx), list_sems.at[0])]
     to_smem[0].start()
-    own_list = pltpu.make_async_copy(mbuf, own_meta, own_list_sem)
-    own_list.start()
     loads[-1].wait()
 
     def moments(g, carry):
@@ -216,27 +214,12 @@
     mine = pltpu.make_async_copy(obuf.at[gz], tiles_all.at[gz], own_sem)
     mine.start()
 
-    own_list.wait()
-    n0 = own_meta[LISTED + nx + 1 + nx]
-    n1 = own_meta[LISTED + nx + 1 + nx + 1]
-
-    def own_item(j, total):
-        e = n0 + j
-        p = jnp.minimum(e, 8 * NEAR - 1)
-        code = own_meta[((p >> 3) << 7) + FAR + (p & 7)]
-        t = code >> 7
-        tile = src[jnp.minimum(code & 127, own - 1)]
-        row = near_row(tile, *(tbuf[c, pl.ds(t, 1), :] for c in range(3)))
-        return total - jnp.where((sub == t) & (e < n1), row, 0.0)
-
-    total = lax.fori_loop(0, OWN // 2, own_item, jnp.zeros((8, 128), jnp.float32), unroll=5)
     for copy in c_copies:
         copy.wait_recv()
     x_copies = [
         sent(cells_all.at[gy], cells_all.at[gy], x_send.at[d], x_recv.at[d], (gx, ys[d], gz))
         for d in range(1, ny)
     ]
-    local[...] = lax.fori_loop(OWN // 2, OWN, own_item, total, unroll=5)
 
     half = nx // 2
     for e in range(1, half - jump + 1):
@@ -289,7 +272,7 @@
     def far_domain(n, carry):
         i = wrap(gx + n, nx)
         bounds = []
-        slot = rows.at[n & 1]
+        slot = rows.at[n & 3]
         for t in range(8):
             at = i * 1024 + t * 128
             f0 = meta[at + LISTED + gx]
@@ -314,17 +297,16 @@
         copy.wait()
     to_smem.clear()
     low_end = nx - jump
-    near_end = low_end + len(first) + 1
-    lax.fori_loop(low_end, near_end, far_domain, 0, unroll=2 if nx > 4 else 1)
-    if near_end < low_end + nx:
-        for d in range(1, nx):
-            if d not in first:
-                m_copy[d].wait_recv()
-                t_copy[d].wait_recv()
-                listed(d)
-        for copy in to_smem:
-            copy.wait()
-        lax.fori_loop(near_end, low_end + nx, far_domain, 0, unroll=2 if nx > 4 else 1)
+    near_end = low_end + (len(first) if len(first) % 4 == 0 else len(first) + 1)
+    lax.fori_loop(low_end, near_end, far_domain, 0, unroll=4 if len(first) % 4 == 0 else 1)
+    for d in range(1, nx):
+        if d not in first:
+            m_copy[d].wait_recv()
+            t_copy[d].wait_recv()
+            listed(d)
+    for copy in to_smem:
+        copy.wait()
+    lax.fori_loop(near_end, low_end + nx, far_domain, 0, unroll=4 if len(first) % 4 == 0 else 1)
     for copy in o_copies:
         copy.wait()
     for copy in [*t_copy.values(), *m_copy.values(), *c_copies, *x_copies]:
@@ -373,7 +355,7 @@
 
 
 def walk_kernel(
-    sizes, meta, cnt, t_all, tiles, table, src, out, todo, rows, tile_buf, sem
+    sizes, meta, cnt, t_all, tiles, table, src, out, todo, rows
 ):
     nx, ny, nz = sizes
     a = lax.axis_index("gx")
@@ -431,10 +413,7 @@
     def own_entry(e, carry):
         code = meta[base + ((e >> 3) << 7) + FAR + (e & 7)]
         t = code >> 7
-        copy = pltpu.make_async_copy(src.at[code & 127], tile_buf, sem)
-        copy.start()
-        copy.wait()
-        row = near_row(tile_buf[...], *(t_all[a, c, pl.ds(t, 1), :] for c in range(3)))
+        row = near_row(src[code & 127], *(t_all[a, c, pl.ds(t, 1), :] for c in range(3)))
         out[a, pl.ds(t, 1), :] -= row
         return carry
 
@@ -442,7 +421,8 @@
 
 
 def return_kernel(
-    sizes, todo, t_all, tiles, part, far_part, local, out, landed, near_rows, mine, send, recv,
+    sizes, todo, lists, t_all, tiles, part, far_part, src,
+    out, landed, near_rows, mine, send, recv,
 ):
     nx, ny, nz = sizes
     gx, gy, gz = (lax.axis_index(n) for n in ALL)
@@ -481,7 +461,21 @@
         )
         copy.start()
         copies.append(copy)
-    summed = mine[gx] + local[...]
+
+    n0 = lists[LISTED + nx + 1 + nx]
+    n1 = lists[LISTED + nx + 1 + nx + 1]
+    sub = iota((8, 128), 0)
+
+    def own_item(j, total):
+        e = n0 + j
+        p = jnp.minimum(e, 8 * NEAR - 1)
+        code = lists[((p >> 3) << 7) + FAR + (p & 7)]
+        t = code >> 7
+        tile = src[code & 127]
+        row = near_row(tile, *(t_all[gx, c, pl.ds(t, 1), :] for c in range(3)))
+        return total - jnp.where((sub == t) & (e < n1), row, 0.0)
+
+    summed = lax.fori_loop(0, OWN, own_item, mine[gx], unroll=4)
     for copy in copies:
         copy.wait()
     for d in range(nx - 1):
@@ -501,28 +495,27 @@
     in_hbm = functools.partial(pltpu.with_memory_space_constraint, memory_space=pltpu.HBM)
     tgt = jnp.transpose(targets.reshape(3, 8, 128), (1, 0, 2))
     src = jnp.transpose(sources.reshape(own, 4, 2, 128), (0, 2, 1, 3)).reshape(own, 8, 128)
-    t_all, meta, tiles_all, cnt, table, local, far_part = pl.pallas_call(
+    t_all, meta, tiles_all, cnt, table, far_part, lists, held = pl.pallas_call(
         functools.partial(gather_kernel, sizes),
         out_shape=(
             shape((nx, 3, 8, 128), f32), shape((nx * 1024,), i32),
             shape((nz, nx * 2, 8, 128), f32), shape((nz, 1, nx * nz), i32),
             shape((ny * nz * own, 128), f32),
-            shape((8, 128), f32), shape((nx, 8, 128), f32),
+            shape((nx, 8, 128), f32), shape((1024,), i32), shape((own, 8, 128), f32),
         ),
         in_specs=[hbm] * 7,
-        out_specs=(vmem,) * 7,
+        out_specs=(vmem,) * 8,
         scratch_shapes=[
             SMEM((2, nx * nz), i32), SMEM((1, nx * nz), i32), VMEM((1, nx * nz), i32),
             SMEM((8,), i32),
             VMEM((8, FAR), i32), VMEM((8, NEAR), i32), VMEM((8, 3, 128), f32),
-            VMEM((own, 8, 128), f32),
-            VMEM((8, 128), i32), VMEM((3, 8, 128), f32), VMEM((1024,), i32),
+            VMEM((8, 128), i32), VMEM((3, 8, 128), f32),
             VMEM((nz, nx * 2, 8, 128), f32), VMEM((own // 8, 128), f32),
-            VMEM((ny, nz, own // 8, 128), f32), VMEM((2, 64, 128), f32),
-            SMEM((nx * 1024,), i32), SMEM((1024,), i32),
+            VMEM((ny, nz, own // 8, 128), f32), VMEM((4, 64, 128), f32),
+            SMEM((nx * 1024,), i32),
             dma((nx,)), dma((nx,)), dma((nx,)), dma((nx,)), dma((nz,)), dma((nz,)),
             dma((nz,)), dma((nz,)), dma((ny,)), dma((ny,)), dma((nz,)), dma((nz,)),
-            dma, dma((nx,)), dma, dma((8,)),
+            dma, dma((nx,)), dma((8,)),
         ],
         compiler_params=pltpu.CompilerParams(
             collective_id=0, has_side_effects=True, vmem_limit_bytes=LIMIT
@@ -534,17 +527,17 @@
     part, todo = pl.pallas_call(
         functools.partial(walk_kernel, sizes),
         out_shape=(shape((nx, 8, 128), f32), shape((nx * 64 + 2,), i32)),
-        in_specs=[smem, smem, vmem, vmem, vmem, hbm],
+        in_specs=[smem, smem, vmem, vmem, vmem, vmem],
         out_specs=(vmem, smem),
-        scratch_shapes=[VMEM((8, 128), f32), VMEM((8, 128), f32), dma],
+        scratch_shapes=[VMEM((8, 128), f32)],
         compiler_params=pltpu.CompilerParams(vmem_limit_bytes=LIMIT),
         name="walk",
-    )(meta, cnt.reshape(-1), t_all, tiles, table, in_hbm(src))
+    )(meta, cnt.reshape(-1), t_all, tiles, table, held)
 
     out = pl.pallas_call(
         functools.partial(return_kernel, sizes),
         out_shape=shape((8, 128), f32),
-        in_specs=[smem, vmem, vmem, vmem, vmem, vmem],
+        in_specs=[smem, smem, vmem, vmem, vmem, vmem, vmem],
         out_specs=vmem,
         scratch_shapes=[
             VMEM((nx - 1, 8, 128), f32), VMEM((128, 128), f32),
@@ -554,7 +547,7 @@
             collective_id=1, has_side_effects=True, vmem_limit_bytes=LIMIT
         ),
         name="bring_back",
-    )(todo, t_all, tiles, part, far_part, local)
+    )(todo, lists, t_all, tiles, part, far_part, held)
     return out.reshape(-1)
 
 

time: 52.6 us -> 52.1 us (level)
    pallas_call x1, Pallas kernels: 33.8 us -> 32.6 us  [body(): pl.pallas_call(functools.partial(gather_kernel, sizes), out_shape=(shape(...]
    pallas_call x1, Pallas kernels: 4.09 us -> 4.95 us  [body(): pl.pallas_call(functools.partial(walk_kernel, sizes), out_shape=(shape((n...]
where the time goes in v1:
time: 52.1 us; the launch traced here: 52.3 us
  Pallas kernels  51.7 us (99%)
  local copies, waits for them, and re-layouts  0.6 us (1%)
    pallas_call x1, Pallas kernels, body(): pl.pallas_call(functools.partial(gather_kernel, sizes), out_shape=(shape(...  32.6 us
    pallas_call x1, Pallas kernels, body(): pl.pallas_call(functools.partial(return_kernel, sizes), out_shape=shape((...  14.1 us
    pallas_call x1, Pallas kernels, body(): pl.pallas_call(functools.partial(walk_kernel, sizes), out_shape=(shape((n...  4.95 us

profile of v1, /device:TPU:8, one launch (start us, length us, event | category | flops | bytes accessed | tf_op | source)
XLA Modules:
  0.0 52.3 jit_solution(18106527266551852888)
XLA Ops:
  0.0 32.6 %gather.1 = (f32[16,3,8,128]{3,2,1,0:T(8,128)S(1)}, s32[16384]{0:T(1024)S(1)}, f32[8,32,8,128]{3,2,1,0:T(8,128)S(1)}, s32[8,1,128]{2,1,0:T(1,128)S(1)}, f32[4096...) custom-call(s32[2,128]{1,0:T(2,128)} %bitcast.20, ...), custom_call_target="tpu_custom_call" | custom-call | tf_op jit(solution)/shard_map/gather/pallas_call | solution.py:498
  32.6 4.9 %walk.1 = (f32[16,8,128]{2,1,0:T(8,128)S(1)}, s32[1026]{0:T(1024)S(1)}) custom-call(s32[16384]{0:T(1024)S(1)} %get-tuple-element.15.meta, s32[1024]{0:T(1024)S(1)} %bitcast.17, f32[16,3,8,128]{3,2,1,0:T(8,128)S(1)} %get-tuple-element.17.t_all, f32[256,8,128]{2,1,0:T(8,128)S(1)} %bitcast.14, f32[4096,128]{1,0:T(8,128)S(1)} %get-tuple-element.19.table, ...), custom_call_target="tpu_custom_call" | custom-call | tf_op jit(solution)/shard_map/walk/pallas_call | solution.py:527
  37.6 14.1 %bring_back.1 = f32[8,128]{1,0:T(8,128)S(1)} custom-call(s32[1026]{0:T(1024)S(1)} %get-tuple-element.21.todo, s32[1024]{0:T(1024)S(1)} %get-tuple-element.22.lists, f32[16,3,8,128]{3,2,1,0:T(8,128)S(1)} %get-tuple-element.17.t_all, f32[256,8,128]{2,1,0:T(8,128)S(1)} %bitcast.15, f32[16,8,128]{2,1,0:T(8,128)S(1)} %get-tuple-element.23.part, ...), custom_call_target="tpu_custom_call" | custom-call | tf_op jit(solution)/shard_map/bring_back/pallas_call | solution.py:537
  51.7 0.6 %copy.10 = f32[1024]{0:T(1024)} copy(f32[1024]{0:T(1024)S(1)} %bitcast.16) | data formatting | bytes 8192

commit v2 on v1

--- a/solution.py
+++ b/solution.py
@@ -106,7 +106,7 @@
     sizes, send_ids_hbm, send_count_hbm, near_count_hbm, far_hbm, near_hbm, tgt_hbm, src_hbm,
     t_all, meta_all, tiles_all, cnt_all, table, far_out, mbuf, src,
     send_ids, send_count, cnt_buf, near_count, far, near, tgt,
-    ids_buf, tbuf, obuf, cbuf, cells_all, rows, meta,
+    ids_buf, tbuf, obuf, cbuf, cells_all, rows, meta_a, meta_b, meta_c,
     t_send, t_recv, m_send, m_recv, o_send, o_recv, c_send, c_recv, x_send, x_recv, n_send, n_recv,
     own_sem, list_sems, in_sems,
 ):
@@ -114,6 +114,7 @@
     gx, gy, gz = (lax.axis_index(n) for n in ALL)
     own = src.shape[0]
     jump = max(1, nx // 4)
+    metas = (meta_a, meta_b, meta_c)
     barrier = pltpu.get_barrier_semaphore()
     loads = [
         pltpu.make_async_copy(source, dest, in_sems.at[n])
@@ -161,18 +162,8 @@
     lists = sorted_lists(nx, nz, ny * nz * own, own, ids_buf[...], counts)
     for t in range(8):
         mbuf[pl.ds(t * 128, 128)] = lists[t]
-    to_smem = [pltpu.make_async_copy(mbuf, meta_of(meta, gx), list_sems.at[0])]
-    to_smem[0].start()
-    loads[-1].wait()
-
-    def moments(g, carry):
-        group = src[pl.ds(g * 8, 8)]
-        x, y, z, m = ([group[:, h * 4 + r, :] for h in range(2)] for r in range(4))
-        cbuf[pl.ds(g, 1), :] = cell_row(x, y, z, m)
-        return carry
-
-    lax.fori_loop(0, own // 8, moments, 0, unroll=2)
-
+    own_copy = pltpu.make_async_copy(mbuf, meta_of(metas[0], gx), list_sems.at[0])
+    own_copy.start()
     def gather_tiles(dz):
         k = zs[dz]
 
@@ -192,6 +183,14 @@
         device = (xs[d], gy, gz)
         m_copy[d] = sent(mbuf, meta_of(meta_all, gx), m_send.at[d], m_recv.at[d], device)
         t_copy[d] = sent(tbuf, t_all.at[gx], t_send.at[d], t_recv.at[d], device)
+    loads[-1].wait()
+
+    def moments(g, carry):
+        x, y, z, m = ([src[pl.ds(g * 8, 8), h * 4 + r, :] for h in range(2)] for r in range(4))
+        cbuf[pl.ds(g, 1), :] = cell_row(x, y, z, m)
+        return carry
+
+    lax.fori_loop(0, own // 8, moments, 0, unroll=2)
     c_copies = [
         sent(cbuf, cells_all.at[gy, gz], c_send.at[d], c_recv.at[d], (gx, gy, zs[d]))
         for d in range(1, nz)
@@ -238,18 +237,28 @@
                 ahead = of(ref, xs[jump])
                 copies[down] = sent(ahead, ahead, s_sems.at[down], r_sems.at[down], (xs[nx - e], gy, gz))
 
-    def listed(d):
-        from_d = xs[nx - d]
-        copy = pltpu.make_async_copy(meta_of(meta_all, from_d), meta_of(meta, from_d), list_sems.at[d])
-        copy.start()
-        to_smem.append(copy)
-
+    near_end = nx // 2
+    mid_end = (near_end + nx) // 2
+    stages = (range(0, near_end), range(near_end, mid_end), range(mid_end, nx))
     waited = {jump, nx - jump} if half > jump else set()
-    for d in first:
-        if d not in waited:
-            m_copy[d].wait_recv()
-            t_copy[d].wait_recv()
-        listed(d)
+
+    def arrived(stage):
+        copies = [own_copy] if stage == 0 else []
+        for n in stages[stage]:
+            d = nx - (n + 1) // 2 if n % 2 else n // 2
+            if d == 0:
+                continue
+            if d not in waited:
+                m_copy[d].wait_recv()
+                t_copy[d].wait_recv()
+            copy = pltpu.make_async_copy(
+                meta_of(meta_all, xs[nx - d]), meta_of(metas[stage], xs[nx - d]), list_sems.at[d]
+            )
+            copy.start()
+            copies.append(copy)
+        return copies
+
+    listed = arrived(0)
     for copy in x_copies:
         copy.wait_recv()
     blocks = own // 64
@@ -269,8 +278,8 @@
         [jnp.where(((k & 15) == p) & (k < 48), 1.0, 0.0) for p in range(11)], axis=1
     ).astype(jnp.bfloat16)
 
-    def far_domain(n, carry):
-        i = wrap(gx + n, nx)
+    def far_domain(meta, n, carry):
+        i = wrap(gx + nx + jnp.where((n & 1) == 1, (n + 1) >> 1, -(n >> 1)), nx)
         bounds = []
         slot = rows.at[n & 3]
         for t in range(8):
@@ -293,20 +302,15 @@
         far_out[i] = -jnp.concatenate(values, axis=0)
         return carry
 
-    for copy in to_smem:
-        copy.wait()
-    to_smem.clear()
-    low_end = nx - jump
-    near_end = low_end + (len(first) if len(first) % 4 == 0 else len(first) + 1)
-    lax.fori_loop(low_end, near_end, far_domain, 0, unroll=4 if len(first) % 4 == 0 else 1)
-    for d in range(1, nx):
-        if d not in first:
-            m_copy[d].wait_recv()
-            t_copy[d].wait_recv()
-            listed(d)
-    for copy in to_smem:
-        copy.wait()
-    lax.fori_loop(near_end, low_end + nx, far_domain, 0, unroll=4 if len(first) % 4 == 0 else 1)
+    for stage, span in enumerate(stages):
+        for copy in listed:
+            copy.wait()
+        lax.fori_loop(
+            span.start, span.stop, functools.partial(far_domain, metas[stage]), 0,
+            unroll=min(4, max(1, len(span))),
+        )
+        if stage < 2:
+            listed = arrived(stage + 1)
     for copy in o_copies:
         copy.wait()
     for copy in [*t_copy.values(), *m_copy.values(), *c_copies, *x_copies]:
@@ -512,7 +516,7 @@
             VMEM((8, 128), i32), VMEM((3, 8, 128), f32),
             VMEM((nz, nx * 2, 8, 128), f32), VMEM((own // 8, 128), f32),
             VMEM((ny, nz, own // 8, 128), f32), VMEM((4, 64, 128), f32),
-            SMEM((nx * 1024,), i32),
+            SMEM((nx * 1024,), i32), SMEM((nx * 1024,), i32), SMEM((nx * 1024,), i32),
             dma((nx,)), dma((nx,)), dma((nx,)), dma((nx,)), dma((nz,)), dma((nz,)),
             dma((nz,)), dma((nz,)), dma((ny,)), dma((ny,)), dma((nz,)), dma((nz,)),
             dma, dma((nx,)), dma((8,)),

time: 52.1 us -> 54.1 us (1.038); the launches traced: 52.3 us -> 53.5 us
  Pallas kernels: 51.7 us -> 52.9 us
    pallas_call x1, Pallas kernels: 32.6 us -> 35 us  [body(): pl.pallas_call(functools.partial(gather_kernel, sizes), out_shape=(shape(...]
    pallas_call x1, Pallas kernels: 4.95 us -> 3.82 us  [body(): pl.pallas_call(functools.partial(walk_kernel, sizes), out_shape=(shape((n...]
where the time goes in v2:
time: 54.1 us; the launch traced here: 53.5 us
  Pallas kernels  52.9 us (98%)
  local copies, waits for them, and re-layouts  0.6 us (1%)
    pallas_call x1, Pallas kernels, body(): pl.pallas_call(functools.partial(gather_kernel, sizes), out_shape=(shape(...  35 us
    pallas_call x1, Pallas kernels, body(): pl.pallas_call(functools.partial(return_kernel, sizes), out_shape=shape((...  14.1 us
    pallas_call x1, Pallas kernels, body(): pl.pallas_call(functools.partial(walk_kernel, sizes), out_shape=(shape((n...  3.82 us

profile of v2, /device:TPU:8, one launch (start us, length us, event | category | flops | bytes accessed | tf_op | source)
XLA Modules:
  0.0 53.5 jit_solution(17738124303652524331)
XLA Ops:
  0.0 35.0 %gather.1 = (f32[16,3,8,128]{3,2,1,0:T(8,128)S(1)}, s32[16384]{0:T(1024)S(1)}, f32[8,32,8,128]{3,2,1,0:T(8,128)S(1)}, s32[8,1,128]{2,1,0:T(1,128)S(1)}, f32[4096...) custom-call(s32[2,128]{1,0:T(2,128)} %bitcast.20, ...), custom_call_target="tpu_custom_call" | custom-call | tf_op jit(solution)/shard_map/gather/pallas_call | solution.py:502
  35.0 3.8 %walk.1 = (f32[16,8,128]{2,1,0:T(8,128)S(1)}, s32[1026]{0:T(1024)S(1)}) custom-call(s32[16384]{0:T(1024)S(1)} %get-tuple-element.15.meta, s32[1024]{0:T(1024)S(1)} %bitcast.17, f32[16,3,8,128]{3,2,1,0:T(8,128)S(1)} %get-tuple-element.17.t_all, f32[256,8,128]{2,1,0:T(8,128)S(1)} %bitcast.14, f32[4096,128]{1,0:T(8,128)S(1)} %get-tuple-element.19.table, ...), custom_call_target="tpu_custom_call" | custom-call | tf_op jit(solution)/shard_map/walk/pallas_call | solution.py:531
  38.8 14.1 %bring_back.1 = f32[8,128]{1,0:T(8,128)S(1)} custom-call(s32[1026]{0:T(1024)S(1)} %get-tuple-element.21.todo, s32[1024]{0:T(1024)S(1)} %get-tuple-element.22.lists, f32[16,3,8,128]{3,2,1,0:T(8,128)S(1)} %get-tuple-element.17.t_all, f32[256,8,128]{2,1,0:T(8,128)S(1)} %bitcast.15, f32[16,8,128]{2,1,0:T(8,128)S(1)} %get-tuple-element.23.part, ...), custom_call_target="tpu_custom_call" | custom-call | tf_op jit(solution)/shard_map/bring_back/pallas_call | solution.py:541
  52.9 0.6 %copy.10 = f32[1024]{0:T(1024)} copy(f32[1024]{0:T(1024)S(1)} %bitcast.16) | data formatting | bytes 8192

commit v3 on v2

--- a/solution.py
+++ b/solution.py
@@ -164,6 +164,18 @@
         mbuf[pl.ds(t * 128, 128)] = lists[t]
     own_copy = pltpu.make_async_copy(mbuf, meta_of(metas[0], gx), list_sems.at[0])
     own_copy.start()
+    loads[-1].wait()
+    flat = src.reshape(own * 8, 128)
+
+    def moments(g, carry):
+        x, y, z, m = (
+            [flat[pl.ds(g * 64 + h * 4 + r, 8, stride=8), :] for h in range(2)] for r in range(4)
+        )
+        cbuf[pl.ds(g, 1), :] = cell_row(x, y, z, m)
+        return carry
+
+    lax.fori_loop(0, own // 8, moments, 0, unroll=4)
+
     def gather_tiles(dz):
         k = zs[dz]
 
@@ -183,14 +195,6 @@
         device = (xs[d], gy, gz)
         m_copy[d] = sent(mbuf, meta_of(meta_all, gx), m_send.at[d], m_recv.at[d], device)
         t_copy[d] = sent(tbuf, t_all.at[gx], t_send.at[d], t_recv.at[d], device)
-    loads[-1].wait()
-
-    def moments(g, carry):
-        x, y, z, m = ([src[pl.ds(g * 8, 8), h * 4 + r, :] for h in range(2)] for r in range(4))
-        cbuf[pl.ds(g, 1), :] = cell_row(x, y, z, m)
-        return carry
-
-    lax.fori_loop(0, own // 8, moments, 0, unroll=2)
     c_copies = [
         sent(cbuf, cells_all.at[gy, gz], c_send.at[d], c_recv.at[d], (gx, gy, zs[d]))
         for d in range(1, nz)
@@ -359,16 +363,26 @@
 
 
 def walk_kernel(
-    sizes, meta, cnt, t_all, tiles, table, src, out, todo, rows
+    sizes, meta_in, cnt_in, lists_in, t_all, tiles, table, src,
+    out, todo, rows, meta_a, meta_b, meta_c, meta_d, cnt, lists, in_sems,
 ):
     nx, ny, nz = sizes
     a = lax.axis_index("gx")
     gz = lax.axis_index("gz")
+    near_base = LISTED + nx + 1
+    metas = (meta_a, meta_b, meta_c, meta_d)
+    each = meta_a.shape[0] // 1024
+    copies = [pltpu.make_async_copy(cnt_in, cnt, in_sems.at[4])]
+    for q in range(nx // each):
+        part = meta_in.at[pl.ds(q * each * 1024, each * 1024)]
+        copies.append(pltpu.make_async_copy(part, metas[q], in_sems.at[q]))
+    copies.append(pltpu.make_async_copy(lists_in, lists, in_sems.at[5]))
+    for copy in copies:
+        copy.start()
     out[...] = jnp.zeros_like(out)
-    near_base = LISTED + nx + 1
-
-    def domain(i, found):
-        base = i * 1024
+
+    def domain(meta, q, i, found):
+        base = (i - q * each) * 1024
         n0 = meta[base + near_base + a]
         n1 = meta[base + near_base + a + 1]
 
@@ -401,7 +415,13 @@
 
         return lax.fori_loop(n0, n1, entry, found)
 
-    found = lax.fori_loop(0, nx, domain, jnp.int32(0))
+    copies[0].wait()
+    found = jnp.int32(0)
+    for q in range(nx // each):
+        copies[q + 1].wait()
+        step = functools.partial(domain, metas[q], q)
+        found = lax.fori_loop(q * each, (q + 1) * each, step, found)
+    copies[-1].wait()
     todo[nx * 64 + 1] = found
 
     def away(n, carry):
@@ -412,21 +432,20 @@
         return carry
 
     lax.fori_loop(AWAY, found, away, 0)
-    base = a * 1024
 
     def own_entry(e, carry):
-        code = meta[base + ((e >> 3) << 7) + FAR + (e & 7)]
+        code = lists[((e >> 3) << 7) + FAR + (e & 7)]
         t = code >> 7
         row = near_row(src[code & 127], *(t_all[a, c, pl.ds(t, 1), :] for c in range(3)))
         out[a, pl.ds(t, 1), :] -= row
         return carry
 
-    lax.fori_loop(meta[base + near_base + nx] + OWN, meta[base + near_base + nx + 1], own_entry, 0)
+    lax.fori_loop(lists[near_base + nx] + OWN, lists[near_base + nx + 1], own_entry, 0)
 
 
 def return_kernel(
-    sizes, todo, lists, t_all, tiles, part, far_part, src,
-    out, landed, near_rows, mine, send, recv,
+    sizes, todo_in, lists_in, t_all, tiles, part, far_part, src,
+    out, landed, near_rows, mine, todo, lists, send, recv, in_sems,
 ):
     nx, ny, nz = sizes
     gx, gy, gz = (lax.axis_index(n) for n in ALL)
@@ -436,6 +455,12 @@
     for d in far_first:
         pl.semaphore_signal(barrier, inc=1, device_id=(xs[d], gy, gz), device_id_type=MESH)
     lane = iota((8, 128), 1)
+    todo_copy = pltpu.make_async_copy(todo_in, todo, in_sems.at[0])
+    lists_copy = pltpu.make_async_copy(lists_in, lists, in_sems.at[1])
+    todo_copy.start()
+    lists_copy.start()
+    todo_copy.wait()
+    lists_copy.wait()
     found = todo[nx * 64 + 1]
 
     def near(j, ids):
@@ -531,21 +556,25 @@
     part, todo = pl.pallas_call(
         functools.partial(walk_kernel, sizes),
         out_shape=(shape((nx, 8, 128), f32), shape((nx * 64 + 2,), i32)),
-        in_specs=[smem, smem, vmem, vmem, vmem, vmem],
+        in_specs=[vmem] * 7,
         out_specs=(vmem, smem),
-        scratch_shapes=[VMEM((8, 128), f32)],
+        scratch_shapes=[
+            VMEM((8, 128), f32), *[SMEM((max(1, nx // 4) * 1024,), i32)] * 4,
+            SMEM((nz * nx * nz,), i32), SMEM((1024,), i32), dma((6,)),
+        ],
         compiler_params=pltpu.CompilerParams(vmem_limit_bytes=LIMIT),
         name="walk",
-    )(meta, cnt.reshape(-1), t_all, tiles, table, held)
+    )(meta, cnt.reshape(-1), lists, t_all, tiles, table, held)
 
     out = pl.pallas_call(
         functools.partial(return_kernel, sizes),
         out_shape=shape((8, 128), f32),
-        in_specs=[smem, smem, vmem, vmem, vmem, vmem, vmem],
+        in_specs=[vmem] * 7,
         out_specs=vmem,
         scratch_shapes=[
             VMEM((nx - 1, 8, 128), f32), VMEM((128, 128), f32),
-            VMEM((nx, 8, 128), f32), dma((nx,)), dma((nx,)),
+            VMEM((nx, 8, 128), f32), SMEM((nx * 64 + 2,), i32), SMEM((1024,), i32),
+            dma((nx,)), dma((nx,)), dma((2,)),
         ],
         compiler_params=pltpu.CompilerParams(
             collective_id=1, has_side_effects=True, vmem_limit_bytes=LIMIT

time: 54.1 us -> 50.9 us (0.941); the launches traced: 53.5 us -> 51.1 us
  Pallas kernels: 52.9 us -> 50.4 us
    pallas_call x1, Pallas kernels: 35 us -> 33.2 us  [body(): pl.pallas_call(functools.partial(gather_kernel, sizes), out_shape=(shape(...]
    pallas_call x1, Pallas kernels: 14.1 us -> 13.4 us  [body(): pl.pallas_call(functools.partial(return_kernel, sizes), out_shape=shape((...]
where the time goes in v3:
time: 50.9 us; the launch traced here: 51.1 us
  Pallas kernels  50.4 us (99%)
  local copies, waits for them, and re-layouts  0.6 us (1%)
    pallas_call x1, Pallas kernels, body(): pl.pallas_call(functools.partial(gather_kernel, sizes), out_shape=(shape(...  33.2 us
    pallas_call x1, Pallas kernels, body(): pl.pallas_call(functools.partial(return_kernel, sizes), out_shape=shape((...  13.4 us
    pallas_call x1, Pallas kernels, body(): pl.pallas_call(functools.partial(walk_kernel, sizes), out_shape=(shape((n...  3.8 us

profile of v3, /device:TPU:8, one launch (start us, length us, event | category | flops | bytes accessed | tf_op | source)
XLA Modules:
  0.0 51.1 jit_solution(12001367734412996178)
XLA Ops:
  0.0 33.2 %gather.1 = (f32[16,3,8,128]{3,2,1,0:T(8,128)S(1)}, s32[16384]{0:T(1024)S(1)}, f32[8,32,8,128]{3,2,1,0:T(8,128)S(1)}, s32[8,1,128]{2,1,0:T(1,128)S(1)}, f32[4096...) custom-call(s32[2,128]{1,0:T(2,128)} %bitcast.20, ...), custom_call_target="tpu_custom_call" | custom-call | tf_op jit(solution)/shard_map/gather/pallas_call | solution.py:527
  33.2 3.8 %walk.1 = (f32[16,8,128]{2,1,0:T(8,128)S(1)}, s32[1026]{0:T(1024)S(1)}) custom-call(s32[16384]{0:T(1024)S(1)} %get-tuple-element.15.meta_in, s32[1024]{0:T(1024)S(1)} %bitcast.17, s32[1024]{0:T(1024)S(1)} %get-tuple-element.17.lists_in, f32[16,3,8,128]{3,2,1,0:T(8,128)S(1)} %get-tuple-element.18.t_all, f32[256,8,128]{2,1,0:T(8,128)S(1)} %bitcast.14, ...), custom_call_target="tpu_custom_call" | custom-call | tf_op jit(solution)/shard_map/walk/pallas_call | solution.py:556
  37.0 13.4 %bring_back.1 = f32[8,128]{1,0:T(8,128)S(1)} custom-call(s32[1026]{0:T(1024)S(1)} %get-tuple-element.22.todo_in, s32[1024]{0:T(1024)S(1)} %get-tuple-element.17.lists_in, f32[16,3,8,128]{3,2,1,0:T(8,128)S(1)} %get-tuple-element.18.t_all, f32[256,8,128]{2,1,0:T(8,128)S(1)} %bitcast.15, f32[16,8,128]{2,1,0:T(8,128)S(1)} %get-tuple-element.23.part, ...), custom_call_target="tpu_custom_call" | custom-call | tf_op jit(solution)/shard_map/bring_back/pallas_call | solution.py:569
  50.5 0.6 %copy.10 = f32[1024]{0:T(1024)} copy(f32[1024]{0:T(1024)S(1)} %bitcast.16) | data formatting | bytes 8192

commit v4 on v3

--- a/solution.py
+++ b/solution.py
@@ -68,8 +68,10 @@
     near_rows = zero
     for t in range(8):
         near_rows = jnp.where(sub == t, pltpu.roll(near_list, (FAR - 8 * t) % 128, 1), near_rows)
-    most = pltpu.roll(far_start, 127, 1) - far_start
-    most = jnp.broadcast_to(jnp.max(most, axis=0, keepdims=True), (8, 128))
+    length = pltpu.roll(far_start, 127, 1) - far_start
+    top = jnp.max(length * 8 + sub, axis=0, keepdims=True) & 7
+    most = jnp.sum(jnp.where(length > 8, 1, 0), axis=0, keepdims=True) * 8 + top
+    most = jnp.broadcast_to(most, (8, 128))
     most = pltpu.roll(most, most_base - far_base, 1)
     out = jnp.where(is_far, far_list, jnp.where(is_near, near_rows, far_start + near_start))
     return jnp.where(lane >= most_base, most, out)
@@ -386,26 +388,30 @@
         n0 = meta[base + near_base + a]
         n1 = meta[base + near_base + a + 1]
 
-        @pl.when(meta[base + LISTED + 2 * nx + 3 + a] > 8)
+        def bucket(t, carry):
+            at = base + t * 128
+            f0 = meta[at + LISTED + a]
+            f1 = meta[at + LISTED + a + 1]
+            tx, ty, tz = (t_all[i, c, pl.ds(t, 1), :] for c in range(3))
+
+            def chunk(n, carry):
+                start = f0 + n * 8
+                for u in range(8):
+                    rows[u : u + 1, :] = table[pl.ds(meta[at + start + u], 1), :]
+                v = rows[...]
+                p = lambda n: jnp.broadcast_to(v[:, n : n + 1], (8, 128))
+                out[i, pl.ds(t, 1), :] -= far_value(p, f1 - start, tx, ty, tz)
+                return carry
+
+            return lax.fori_loop(1, (f1 - f0 + 7) >> 3, chunk, carry)
+
+        longer = meta[base + LISTED + 2 * nx + 3 + a]
+
+        @pl.when(longer >= 8)
         def _():
-            def bucket(t, carry):
-                at = base + t * 128
-                f0 = meta[at + LISTED + a]
-                f1 = meta[at + LISTED + a + 1]
-                tx, ty, tz = (t_all[i, c, pl.ds(t, 1), :] for c in range(3))
-
-                def chunk(n, carry):
-                    start = f0 + n * 8
-                    for u in range(8):
-                        rows[u : u + 1, :] = table[pl.ds(meta[at + start + u], 1), :]
-                    v = rows[...]
-                    p = lambda n: jnp.broadcast_to(v[:, n : n + 1], (8, 128))
-                    out[i, pl.ds(t, 1), :] -= far_value(p, f1 - start, tx, ty, tz)
-                    return carry
-
-                return lax.fori_loop(1, (f1 - f0 + 7) >> 3, chunk, carry)
-
-            lax.fori_loop(0, 8, bucket, 0)
+            alone = longer < 16
+            begin = jnp.where(alone, longer & 7, 0)
+            lax.fori_loop(begin, jnp.where(alone, begin + 1, 8), bucket, 0)
 
         def entry(e, found):
             code = meta[base + ((e >> 3) << 7) + FAR + (e & 7)]

time: 50.9 us -> 50.5 us (level); the launches traced: 51.1 us -> 50.1 us
  Pallas kernels: 50.4 us -> 49.5 us
    pallas_call x1, Pallas kernels: 3.8 us -> 2.85 us  [body(): pl.pallas_call(functools.partial(walk_kernel, sizes), out_shape=(shape((n...]
where the time goes in v4:
time: 50.5 us; the launch traced here: 50.1 us
  Pallas kernels  49.5 us (98%)
  local copies, waits for them, and re-layouts  0.6 us (1%)
    pallas_call x1, Pallas kernels, body(): pl.pallas_call(functools.partial(gather_kernel, sizes), out_shape=(shape(...  33.2 us
    pallas_call x1, Pallas kernels, body(): pl.pallas_call(functools.partial(return_kernel, sizes), out_shape=shape((...  13.4 us
    pallas_call x1, Pallas kernels, body(): pl.pallas_call(functools.partial(walk_kernel, sizes), out_shape=(shape((n...  2.85 us

profile of v4, /device:TPU:8, one launch (start us, length us, event | category | flops | bytes accessed | tf_op | source)
XLA Modules:
  0.0 50.1 jit_solution(471491467561821158)
XLA Ops:
  0.0 33.2 %gather.1 = (f32[16,3,8,128]{3,2,1,0:T(8,128)S(1)}, s32[16384]{0:T(1024)S(1)}, f32[8,32,8,128]{3,2,1,0:T(8,128)S(1)}, s32[8,1,128]{2,1,0:T(1,128)S(1)}, f32[4096...) custom-call(s32[2,128]{1,0:T(2,128)} %bitcast.20, ...), custom_call_target="tpu_custom_call" | custom-call | tf_op jit(solution)/shard_map/gather/pallas_call | solution.py:533
  33.2 2.9 %walk.1 = (f32[16,8,128]{2,1,0:T(8,128)S(1)}, s32[1026]{0:T(1024)S(1)}) custom-call(s32[16384]{0:T(1024)S(1)} %get-tuple-element.15.meta_in, s32[1024]{0:T(1024)S(1)} %bitcast.17, s32[1024]{0:T(1024)S(1)} %get-tuple-element.17.lists_in, f32[16,3,8,128]{3,2,1,0:T(8,128)S(1)} %get-tuple-element.18.t_all, f32[256,8,128]{2,1,0:T(8,128)S(1)} %bitcast.14, ...), custom_call_target="tpu_custom_call" | custom-call | tf_op jit(solution)/shard_map/walk/pallas_call | solution.py:562
  36.1 13.4 %bring_back.1 = f32[8,128]{1,0:T(8,128)S(1)} custom-call(s32[1026]{0:T(1024)S(1)} %get-tuple-element.22.todo_in, s32[1024]{0:T(1024)S(1)} %get-tuple-element.17.lists_in, f32[16,3,8,128]{3,2,1,0:T(8,128)S(1)} %get-tuple-element.18.t_all, f32[256,8,128]{2,1,0:T(8,128)S(1)} %bitcast.15, f32[16,8,128]{2,1,0:T(8,128)S(1)} %get-tuple-element.23.part, ...), custom_call_target="tpu_custom_call" | custom-call | tf_op jit(solution)/shard_map/bring_back/pallas_call | solution.py:575
  49.5 0.6 %copy.10 = f32[1024]{0:T(1024)} copy(f32[1024]{0:T(1024)S(1)} %bitcast.16) | data formatting | bytes 8192

commit v5 on v4

--- a/solution.py
+++ b/solution.py
@@ -207,12 +207,23 @@
     ]
     cells_all[gy, gz] = cbuf[...]
     o_copies = []
-    gather_tiles(1)
-    for d in range(1, nz):
-        gather_tiles((d + 1) % nz)
+    middle = nz // 2
+    order = [middle, *(d for d in (2, nz - 2, 3) if d != middle and 0 < d < nz)]
+    order = list(dict.fromkeys(order))
+    later = [d for d in range(1, nz) if d not in order]
+
+    def send_tiles(d):
         o_copies.append(
             sent(obuf.at[zs[d]], tiles_all.at[gz], o_send.at[d], o_recv.at[d], (gx, gy, zs[d]))
         )
+
+    gather_tiles(order[0])
+    for d, following in zip(order, [*order[1:], None]):
+        if following:
+            gather_tiles(following)
+        send_tiles(d)
+    for d in [*later, 0]:
+        gather_tiles(d)
     t_all[gx] = tbuf[...]
     meta_all[pl.ds(pl.multiple_of(gx * 1024, 1024), 1024)] = mbuf[...]
     cnt_all[gz] = cnt_buf[...]
@@ -242,6 +253,9 @@
             if e < half - jump or copies is m_copy:
                 ahead = of(ref, xs[jump])
                 copies[down] = sent(ahead, ahead, s_sems.at[down], r_sems.at[down], (xs[nx - e], gy, gz))
+
+    for d in later:
+        send_tiles(d)
 
     near_end = nx // 2
     mid_end = (near_end + nx) // 2

time: 50.5 us -> 47.9 us (0.949)
  the two profiles are of different devices: /device:TPU:8 before, /device:TPU:1 now
where the time goes in v5:
time: 47.9 us; the launch traced here: 47.8 us
  Pallas kernels  47.1 us (98%)
  local copies, waits for them, and re-layouts  0.6 us (1%)
    pallas_call x1, Pallas kernels, body(): pl.pallas_call(functools.partial(gather_kernel, sizes), out_shape=(shape(...  31.9 us
    pallas_call x1, Pallas kernels, body(): pl.pallas_call(functools.partial(return_kernel, sizes), out_shape=shape((...  12.4 us
    pallas_call x1, Pallas kernels, body(): pl.pallas_call(functools.partial(walk_kernel, sizes), out_shape=(shape((n...  2.91 us

profile of v5, /device:TPU:1, one launch (start us, length us, event | category | flops | bytes accessed | tf_op | source)
XLA Modules:
  0.0 47.8 jit_solution(15752981050997882383)
XLA Ops:
  0.0 31.9 %gather.1 = (f32[16,3,8,128]{3,2,1,0:T(8,128)S(1)}, s32[16384]{0:T(1024)S(1)}, f32[8,32,8,128]{3,2,1,0:T(8,128)S(1)}, s32[8,1,128]{2,1,0:T(1,128)S(1)}, f32[4096...) custom-call(s32[2,128]{1,0:T(2,128)} %bitcast.20, ...), custom_call_target="tpu_custom_call" | custom-call | tf_op jit(solution)/shard_map/gather/pallas_call | solution.py:547
  31.9 2.9 %walk.1 = (f32[16,8,128]{2,1,0:T(8,128)S(1)}, s32[1026]{0:T(1024)S(1)}) custom-call(s32[16384]{0:T(1024)S(1)} %get-tuple-element.15.meta_in, s32[1024]{0:T(1024)S(1)} %bitcast.17, s32[1024]{0:T(1024)S(1)} %get-tuple-element.17.lists_in, f32[16,3,8,128]{3,2,1,0:T(8,128)S(1)} %get-tuple-element.18.t_all, f32[256,8,128]{2,1,0:T(8,128)S(1)} %bitcast.14, ...), custom_call_target="tpu_custom_call" | custom-call | tf_op jit(solution)/shard_map/walk/pallas_call | solution.py:576
  34.8 12.4 %bring_back.1 = f32[8,128]{1,0:T(8,128)S(1)} custom-call(s32[1026]{0:T(1024)S(1)} %get-tuple-element.22.todo_in, s32[1024]{0:T(1024)S(1)} %get-tuple-element.17.lists_in, f32[16,3,8,128]{3,2,1,0:T(8,128)S(1)} %get-tuple-element.18.t_all, f32[256,8,128]{2,1,0:T(8,128)S(1)} %bitcast.15, f32[16,8,128]{2,1,0:T(8,128)S(1)} %get-tuple-element.23.part, ...), custom_call_target="tpu_custom_call" | custom-call | tf_op jit(solution)/shard_map/bring_back/pallas_call | solution.py:589
  47.2 0.6 %copy.10 = f32[1024]{0:T(1024)} copy(f32[1024]{0:T(1024)S(1)} %bitcast.16) | data formatting | bytes 8192

commit v6 on v5

--- a/solution.py
+++ b/solution.py
@@ -193,10 +193,15 @@
     pl.semaphore_wait(barrier, len(greeted))
 
     t_copy, m_copy = {}, {}
-    for d in first:
+
+    def send_own(d):
         device = (xs[d], gy, gz)
         m_copy[d] = sent(mbuf, meta_of(meta_all, gx), m_send.at[d], m_recv.at[d], device)
         t_copy[d] = sent(tbuf, t_all.at[gx], t_send.at[d], t_recv.at[d], device)
+
+    to_forward = [d for d in first if min(d, nx - d) == jump]
+    for d in to_forward:
+        send_own(d)
     c_copies = [
         sent(cbuf, cells_all.at[gy, gz], c_send.at[d], c_recv.at[d], (gx, gy, zs[d]))
         for d in range(1, nz)
@@ -222,6 +227,9 @@
         if following:
             gather_tiles(following)
         send_tiles(d)
+    for d in first:
+        if d not in to_forward:
+            send_own(d)
     for d in [*later, 0]:
         gather_tiles(d)
     t_all[gx] = tbuf[...]

time: 47.9 us -> 47.8 us (level)
  the two profiles are of different devices: /device:TPU:1 before, /device:TPU:32 now
where the time goes in v6:
time: 47.8 us; the launch traced here: 47.6 us
  Pallas kernels  47 us (98%)
  local copies, waits for them, and re-layouts  0.6 us (1%)
    pallas_call x1, Pallas kernels, body(): pl.pallas_call(functools.partial(gather_kernel, sizes), out_shape=(shape(...  30.5 us
    pallas_call x1, Pallas kernels, body(): pl.pallas_call(functools.partial(return_kernel, sizes), out_shape=shape((...  13.4 us
    pallas_call x1, Pallas kernels, body(): pl.pallas_call(functools.partial(walk_kernel, sizes), out_shape=(shape((n...  3.09 us

profile of v6, /device:TPU:32, one launch (start us, length us, event | category | flops | bytes accessed | tf_op | source)
XLA Modules:
  0.0 47.6 jit_solution(3226158467381677228)
XLA Ops:
  0.0 30.5 %gather.1 = (f32[16,3,8,128]{3,2,1,0:T(8,128)S(1)}, s32[16384]{0:T(1024)S(1)}, f32[8,32,8,128]{3,2,1,0:T(8,128)S(1)}, s32[8,1,128]{2,1,0:T(1,128)S(1)}, f32[4096...) custom-call(s32[2,128]{1,0:T(2,128)} %bitcast.20, ...), custom_call_target="tpu_custom_call" | custom-call | tf_op jit(solution)/shard_map/gather/pallas_call | solution.py:555
  30.5 3.1 %walk.1 = (f32[16,8,128]{2,1,0:T(8,128)S(1)}, s32[1026]{0:T(1024)S(1)}) custom-call(s32[16384]{0:T(1024)S(1)} %get-tuple-element.15.meta_in, s32[1024]{0:T(1024)S(1)} %bitcast.17, s32[1024]{0:T(1024)S(1)} %get-tuple-element.17.lists_in, f32[16,3,8,128]{3,2,1,0:T(8,128)S(1)} %get-tuple-element.18.t_all, f32[256,8,128]{2,1,0:T(8,128)S(1)} %bitcast.14, ...), custom_call_target="tpu_custom_call" | custom-call | tf_op jit(solution)/shard_map/walk/pallas_call | solution.py:584
  33.6 13.4 %bring_back.1 = f32[8,128]{1,0:T(8,128)S(1)} custom-call(s32[1026]{0:T(1024)S(1)} %get-tuple-element.22.todo_in, s32[1024]{0:T(1024)S(1)} %get-tuple-element.17.lists_in, f32[16,3,8,128]{3,2,1,0:T(8,128)S(1)} %get-tuple-element.18.t_all, f32[256,8,128]{2,1,0:T(8,128)S(1)} %bitcast.15, f32[16,8,128]{2,1,0:T(8,128)S(1)} %get-tuple-element.23.part, ...), custom_call_target="tpu_custom_call" | custom-call | tf_op jit(solution)/shard_map/bring_back/pallas_call | solution.py:597
  47.0 0.6 %copy.10 = f32[1024]{0:T(1024)} copy(f32[1024]{0:T(1024)S(1)} %bitcast.16) | data formatting | bytes 8192
